TPU v7x, 512 devices: a whole 4x8x8 slice. The times are simulated.
512 devices in a mesh: replica: 32 (over y, x), owner: 16 (over z, core).
Axes of the slice: x: 4, y: 8, z: 8, core: 2. Of those that a mesh axis runs over, the one named last changes fastest.
Arguments:
- owner_of: int32 [24], replicated, may hold values from 0 to 15, as said below
- grad: bfloat16 [32, 32, 2304, 128], P('replica', 'owner')
- error: bfloat16 [32, 32, 2304, 128], P('replica', 'owner'), may hold values from -4 to 4
- q_prev: float32 [32, 128, 32], P('owner')
- weight: float32 [32, 2304, 128], P('owner', 'replica'), may hold values from -0.125 to 0.125
- momentum: float32 [32, 2304, 128], P('owner', 'replica'), may hold values from -1.2 to 1.2
- vec_grad: bfloat16 [32, 128, 2304], P('replica', 'owner')
- vec_weight: float32 [128, 2304], P('owner', 'replica'), may hold values from 0.5 to 1.5
- vec_mom: float32 [128, 2304], P('owner', 'replica'), may hold values from -1.2 to 1.2
Outputs:
- weight_next: float32 [32, 2304, 128], P('owner', 'replica')
- momentum_next: float32 [32, 2304, 128], P('owner', 'replica')
- error_next: bfloat16 [32, 32, 2304, 128], P('replica', 'owner')
- q_next: float32 [32, 128, 32], P('owner')
- vec_weight_next: float32 [128, 2304], P('owner', 'replica')
- vec_mom_next: float32 [128, 2304], P('owner', 'replica')
Inputs may be any that keep to these rules, and one draw needn't show every extreme that they name: `owner_of`: every owner index appears once or twice; half of them appear twice.
All inputs are finite; a program needn't handle non-finite values.
Results may differ from a plain program's by a relative error of at most 0.001.
Values sent between devices are 32-bit elements; how exact they have to be, the bound alone decides.
A program may use at most 64 MiB of HBM per device.

v0:
```python
import jax
import jax.numpy as jnp
from jax import lax
from jax.sharding import PartitionSpec as P

NS_ITERS = 5


exact_mode = lax.Precision.HIGHEST
clip_limit = 0.1
momentum_decay = 0.9
learn_rate = 0.05


def inverse_root(gram_mat, iterations):
    identity = jnp.eye(gram_mat.shape[-1], dtype=jnp.float32)
    scale_sq = jnp.sqrt(jnp.sum(gram_mat * gram_mat, axis=(1, 2), keepdims=True) + 1e-06)
    current = gram_mat / scale_sq
    inv_root = jnp.broadcast_to(identity, gram_mat.shape)
    for iteration in range(iterations):
        factor_mat = 1.5 * identity - 0.5 * jnp.einsum(
            "sij,sjk->sik", inv_root, current, precision=exact_mode
        )
        current = jnp.einsum("sij,sjk->sik", current, factor_mat, precision=exact_mode)
        inv_root = jnp.einsum("sij,sjk->sik", factor_mat, inv_root, precision=exact_mode)
    return (inv_root, scale_sq)


def on_device(owner_of, grad, error, q_prev, weight, momentum, vec_grad, vec_weight, vec_mom):
    replicas = lax.axis_size("replica")
    owners = lax.axis_size("owner")
    rank_index = lax.axis_index("replica")
    owner_index = lax.axis_index("owner")
    slot_count = grad.shape[1]
    rows_share = weight.shape[1]
    count_own = jnp.sum((owner_of == owner_index).astype(jnp.int32))
    live_slots = jnp.arange(slot_count, dtype=jnp.int32) < count_own
    live_mask = live_slots[:, None, None]
    merged = grad[0].astype(jnp.float32) + error[0].astype(jnp.float32)
    left_terms = jnp.einsum("sdw,swk->sdk", merged, q_prev, precision=exact_mode)
    vec_terms = vec_grad[0].astype(jnp.float32)
    p_sum, vec_sum = lax.psum((left_terms, vec_terms), "replica")
    gram_mat = jnp.einsum("sdi,sdj->sij", p_sum, p_sum, precision=exact_mode)
    inv_root, scale_sq = inverse_root(gram_mat, NS_ITERS)
    p_hat = jnp.einsum("sdi,sij->sdj", p_sum, inv_root, precision=exact_mode) / jnp.sqrt(scale_sq)
    vec_full = vec_sum / replicas
    vec_cols = lax.dynamic_slice_in_dim(vec_full, rank_index * rows_share, rows_share, 1)
    right_terms = jnp.einsum("sdw,sdk->swk", merged, p_hat, precision=exact_mode)
    q_new = lax.psum(right_terms, "replica") / replicas
    approx = jnp.einsum("sdk,swk->sdw", p_hat, q_new, precision=exact_mode)
    error_next = jnp.where(live_mask, (merged - approx).astype(jnp.bfloat16), error[0])
    approx_rows = lax.dynamic_slice_in_dim(approx, rank_index * rows_share, rows_share, 1)
    local_sq = jnp.sum(jnp.where(live_mask, approx * approx, 0.0)) + jnp.sum(vec_full * vec_full)
    total_sq = lax.psum(local_sq, "owner")
    width = merged.shape[1]
    entry_count = float(
        owner_of.shape[0] * width * merged.shape[2] + owners * vec_grad.shape[1] * width
    )
    factor = jnp.minimum(1.0, clip_limit / jnp.sqrt(total_sq / entry_count + 1e-06))
    momentum_next = jnp.where(live_mask, momentum_decay * momentum + factor * approx_rows, momentum)
    weight_next = jnp.where(live_mask, weight - learn_rate * momentum_next, weight)
    q_next = jnp.where(live_mask, q_new, q_prev)
    vec_mom_next = momentum_decay * vec_mom + factor * vec_cols
    vec_weight_next = vec_weight - learn_rate * vec_mom_next
    return (weight_next, momentum_next, error_next[None], q_next, vec_weight_next, vec_mom_next)


def solution(mesh):
    return jax.shard_map(
        on_device,
        mesh=mesh,
        in_specs=(
            P(),
            P("replica", "owner", None, None),
            P("replica", "owner", None, None),
            P("owner", None, None),
            P("owner", "replica", None),
            P("owner", "replica", None),
            P("replica", "owner", None),
            P("owner", "replica"),
            P("owner", "replica"),
        ),
        out_specs=(
            P("owner", "replica", None),
            P("owner", "replica", None),
            P("replica", "owner", None, None),
            P("owner", None, None),
            P("owner", "replica"),
            P("owner", "replica"),
        ),
        check_vma=False,
    )
```

profile of v0, /device:TPU:1, one launch (start us, length us, event | category | flops | bytes accessed | tf_op | source)
XLA Modules:
  0.0 373.0 jit_solution(3170516663309399154)
XLA Ops:
  7.2 1.4 bitcast_convert_fusion
  8.6 5.1 %fusion.1 = f32[2,2304,32]{1,2,0:T(8,128)} fusion(f32[2,128,32]{1,2,0:T(8,128)} %param.12, bf16[1,2,2304,128]{3,2,1,0:T(8,128)(2,1)} %param.10, bf16[1,2,2304,128]{3,2,1,0:T(8,128)(2,1)} %param.11), kind=kOutput, calls=%fused_computation.5 | convolution fusion | flops 228261888 | bytes 2981888 | tf_op jit(solution)/shard_map/sdw,swk->sdk/dot_general | solution.py:40
  13.8 0.6 fusion.22
  14.4 0.6 iota_compare_fusion.1
  15.1 159.0 %all-reduce.3.cloned.1.call-done = (f32[2,2304,32]{1,2,0:T(8,128)}, f32[8,2304]{1,0:T(8,128)}) async-done(((f32[2,2304,32]{1,2,0:T(8,128)}, f32[8,2304]{1,0:T(8,128)}), (f32[2,2304,32]{1,2,0:T(8,128)}, f32[8,2304]{1,0:T(8,128)})) %all-reduce.3.cloned.1.call-update) | async-done | bytes 663568 | tf_op jit(solution)/shard_map/psum | solution.py:42
  174.1 2.1 multiply_reduce_fusion.1
  176.2 0.2 fusion.12
  176.5 0.2 fusion.21
  176.9 0.2 fusion.11
  177.1 0.2 fusion.26
  177.4 0.2 fusion.10
  177.9 0.2 fusion.9
  178.4 0.6 broadcast_multiply_fusion
  179.1 0.2 fusion.8
  179.2 0.2 fusion.31
  179.5 0.6 convolution_divide_fusion
  180.1 1.6 fusion
  181.8 113.6 %psum.29 = f32[2,128,32]{1,2,0:T(8,128)S(1)} all-reduce(f32[2,128,32]{1,2,0:T(8,128)S(1)} %fusion), channel_id=1, replica_groups=mesh['replica'=32,'owner'=16] {'replica'}, use_global_device_ids=true, to_apply=%region_3.0 | all-reduce | flops 8192 | bytes 65536 | tf_op jit(solution)/shard_map/psum | solution.py:49
  295.4 5.9 %select_reduce_fusion = (f32[]{:T(128)}, f32[2,2304,128]{2,1,0:T(8,128)}) fusion(pred[2]{0:T(512)(128)(4,1)S(1)} %iota_compare_fusion.1, f32[2,2304,32]{1,2,0:T(8,128)S(1)} %convolution_divide_fusion, f32[2,128,32]{1,2,0:T(8,128)S(1)} %psum.29), kind=kOutput, calls=%fused_computation.3 | convolution fusion | flops 228270080 | bytes 2981894 | tf_op jit(solution)/shard_map/sdk,swk->sdw/dot_general | solution.py:50
  302.6 0.7 multiply_select_fusion
  303.3 56.5 %psum.31 = f32[]{:T(128)} all-reduce(f32[]{:T(128)S(6)} %add.40), channel_id=1, replica_groups=mesh['replica'=32,'owner'=16] {'owner'}, use_global_device_ids=true, to_apply=%region_7.8 | all-reduce | flops 1 | bytes 8 | tf_op jit(solution)/shard_map/psum | solution.py:54
  360.6 3.2 fusion.3
  363.8 1.6 subtract_select_fusion
  365.5 0.7 multiply_subtract_fusion
  (31 shorter events, 1.1 us)
Async XLA Ops:
  7.2 6.6 %copy-start.9 = (s32[24]{0:T(128)S(1)}, s32[24]{0:T(128)}, u32[]{:S(2)}) copy-start(s32[24]{0:T(128)} %param.9) | copy-start | bytes 292
  7.2 166.9 %all-reduce.3.cloned.1.call-start = ((), (), s32[]{:S(2)}) async-start(), calls=%async_computation | async-start | bytes 1327104 | tf_op jit(solution)/shard_map/psum | solution.py:42
  174.1 4.4 %copy-start.4 = (f32[8,2304]{1,0:T(8,128)S(1)}, f32[8,2304]{1,0:T(8,128)}, u32[]{:S(2)}) copy-start(f32[8,2304]{1,0:T(8,128)} %get-tuple-element.7) | copy-start | bytes 221188
  174.1 5.4 %copy-start.2 = (f32[2,2304,32]{1,2,0:T(8,128)S(1)}, f32[2,2304,32]{1,2,0:T(8,128)}, u32[]{:S(2)}) copy-start(f32[2,2304,32]{1,2,0:T(8,128)} %get-tuple-element.6) | copy-start | bytes 1769476
  174.1 6.0 %copy-start = (bf16[1,2,2304,128]{3,2,1,0:T(8,128)(2,1)S(1)}, bf16[1,2,2304,128]{3,2,1,0:T(8,128)(2,1)}, u32[]{:S(2)}) copy-start(bf16[1,2,2304,128]{3,2,1,0:T(8,128)(2,1)} %param.10) | copy-start | bytes 3538948
  174.1 6.0 %copy-start.1 = (bf16[1,2,2304,128]{3,2,1,0:T(8,128)(2,1)S(1)}, bf16[1,2,2304,128]{3,2,1,0:T(8,128)(2,1)}, u32[]{:S(2)}) copy-start(bf16[1,2,2304,128]{3,2,1,0:T(8,128)(2,1)} %param.11) | copy-start | bytes 3538948
  180.1 122.5 %copy-start.3 = (f32[2,128,32]{1,2,0:T(8,128)S(1)}, f32[2,128,32]{1,2,0:T(8,128)}, u32[]{:S(2)}) copy-start(f32[2,128,32]{1,2,0:T(8,128)} %param.12) | copy-start | bytes 98308
  360.5 3.3 copy-start.5
  360.5 3.3 copy-start.6
  360.6 4.9 %copy-start.7 = (f32[8,72]{1,0:T(8,128)S(1)}, f32[8,72]{1,0:T(8,128)}, u32[]{:S(2)}) copy-start(f32[8,72]{1,0:T(8,128)} %param.16) | copy-start | bytes 6916
  360.6 4.9 %copy-start.8 = (f32[8,72]{1,0:T(8,128)S(1)}, f32[8,72]{1,0:T(8,128)}, u32[]{:S(2)}) copy-start(f32[8,72]{1,0:T(8,128)} %param.17) | copy-start | bytes 6916
Sparse Core Ops, SparseCore 0:
  13.9 160.1 all-reduce.2
where the time goes:
time: 373 us
  blocking collectives  170 us (46%)
  waiting for transfers between devices  159 us (43%)
  matrix products  17.9 us (5%)
  between operations  16.3 us (4%)
  other arithmetic  9.55 us (3%)
    psum x1, waiting for transfers between devices, on_device(): p_sum, vec_sum = lax.psum((left_terms, vec_terms), 'replica')  159 us
    psum x1, blocking collectives, on_device(): q_new = lax.psum(right_terms, 'replica') / replicas  114 us
    psum x1, blocking collectives, on_device(): total_sq = lax.psum(local_sq, 'owner')  56.5 us
  transfers between devices with their start and end apart: 1, of which 1 were waited for; matrix products, arithmetic and copies ran while one was open for 0% of the time, Pallas kernels for 0%

commit v1 on v0

v1 whole, which is shorter than its diff:
```python
import functools

import jax
import jax.numpy as jnp
from jax import lax
from jax.experimental import pallas as pl
from jax.experimental.pallas import tpu as pltpu
from jax.sharding import PartitionSpec as P

MESH = pl.DeviceIdType.MESH
NS_ITERS = 5
NX, NY, NO = 4, 8, 16
clip_limit = 0.1
momentum_decay = 0.9
learn_rate = 0.05
f32, bf16 = jnp.float32, jnp.bfloat16
HIGH = lax.Precision.HIGHEST


def split(a):
    hi = a.astype(bf16)
    return hi, (a - hi.astype(f32)).astype(bf16)


def dot(a, b, dims=((1,), (0,)), precision=None):
    return lax.dot_general(a, b, (dims, ((), ())), precision=precision, preferred_element_type=f32)


def gather_kernel(
    own_ref, grad_ref, err_ref, q_ref, vec_ref,
    pf_ref, b_ref, qt_ref, vs_ref, fac_ref,
    gv, ev, qv, vv, loc, rx0, c0, ry0, own0, gy0, ry1, c1, rx1, own1, gx1,
    vpk, vrx, vc, vry, tt, try_, tx, tf, sc,
    load_sem, send_sem, recv_sem,
    *, entries,
):
    r = lax.axis_index("replica")
    o = lax.axis_index("owner")
    x, y = lax.rem(r, NX), r // NX

    def xpeer(d):
        return (y * NX + lax.rem(x + d, NX), o)

    def ypeer(d):
        return (lax.rem(y + d, NY) * NX + x, o)

    def opeer(d):
        return (r, lax.rem(o + d, NO))

    barrier = pltpu.get_barrier_semaphore()
    peers = [xpeer(d) for d in range(1, NX)] + [ypeer(d) for d in range(1, NY)] + [opeer(d) for d in range(1, NO)]
    for peer in peers:
        pl.semaphore_signal(barrier, inc=1, device_id=peer, device_id_type=MESH)

    loads = []
    for n, (src, dst) in enumerate(
        [(q_ref, qv), (grad_ref.at[0, 0], gv.at[0]), (err_ref.at[0, 0], ev.at[0]),
         (grad_ref.at[0, 1], gv.at[1]), (err_ref.at[0, 1], ev.at[1]), (vec_ref.at[0], vv)]
    ):
        copy = pltpu.make_async_copy(src, dst, load_sem.at[n])
        copy.start()
        loads.append(copy)

    started = []

    def send(src, dst, peer):
        n = len(started)
        copy = pltpu.make_async_remote_copy(
            src_ref=src, dst_ref=dst, send_sem=send_sem.at[n], recv_sem=recv_sem.at[n],
            device_id=peer, device_id_type=MESH,
        )
        copy.start()
        started.append(copy)
        return copy

    def arrive(copies):
        for copy in copies:
            copy.wait_recv()

    lane_block = lax.broadcasted_iota(jnp.int32, (128, 128), 1) // 32
    row_block = lax.broadcasted_iota(jnp.int32, (128, 128), 0) // 32
    lane_k = lax.broadcasted_iota(jnp.int32, (128, 128), 1)
    row_k = lax.broadcasted_iota(jnp.int32, (128, 128), 0)

    def left(s):
        wide = jnp.concatenate([qv[s]] * 4, axis=1)
        hi, lo = split(wide)
        total = None
        for j in range(4):
            keep = lane_block == j
            zero = jnp.zeros_like(hi)
            half = jnp.concatenate([jnp.where(keep, hi, zero), jnp.where(keep, lo, zero)], axis=1)
            rhs = jnp.concatenate([half, half], axis=0)
            rows = slice(576 * j, 576 * j + 576)
            term = dot(jnp.concatenate([gv[s, rows], ev[s, rows]], axis=1), rhs)
            total = term if total is None else total + term
        loc[s] = total[:, :128] + total[:, 128:]

    loads[0].wait()
    loads[1].wait()
    loads[2].wait()
    left(0)
    pl.semaphore_wait(barrier, len(peers))

    x0 = []
    for d in (2, 1, 3):
        to = lax.rem(x + d, NX)
        x0.append(send(loc.at[0, pl.ds(pl.multiple_of(to * 144, 8), 144)], rx0.at[d - 1], xpeer(d)))
    loads[3].wait()
    loads[4].wait()
    left(1)
    y1 = []
    for d in (4, 3, 5, 2, 6, 1, 7):
        to = lax.rem(y + d, NY)
        y1.append(send(loc.at[1, pl.ds(pl.multiple_of(to * 72, 8), 72)], ry1.at[d - 1], ypeer(d)))

    loads[5].wait()
    vall = vv[...].astype(f32)
    for yy in range(NY):
        for xx in range(NX):
            at = 72 * (NX * yy + xx)
            piece = jnp.concatenate([vall[:, at:at + 72], jnp.zeros((8, 56), f32)], axis=1)
            vpk[xx * NY + yy] = piece

    arrive(x0)
    acc = loc[0, pl.ds(pl.multiple_of(x * 144, 8), 144)] + rx0[0] + rx0[1] + rx0[2]
    pad = jnp.zeros((6, 128), f32)
    for yy in range(NY):
        c0[yy] = jnp.concatenate([acc[18 * yy:18 * yy + 18], pad], axis=0)
    y0 = []
    for d in (4, 3, 5, 2, 6, 1, 7):
        y0.append(send(c0.at[lax.rem(y + d, NY)], ry0.at[d - 1], ypeer(d)))

    arrive(y1)
    acc = loc[1, pl.ds(pl.multiple_of(y * 72, 8), 72)]
    for d in range(7):
        acc = acc + ry1[d]
    for xx in range(NX):
        c1[xx] = jnp.concatenate([acc[18 * xx:18 * xx + 18], pad], axis=0)
    x1 = []
    for d in (2, 1, 3):
        x1.append(send(c1.at[lax.rem(x + d, NX)], rx1.at[d - 1], xpeer(d)))

    vx = []
    for d in (2, 1, 3):
        to = lax.rem(x + d, NX)
        vx.append(send(vpk.at[pl.ds(to * NY, NY)], vrx.at[d - 1], xpeer(d)))

    arrive(y0)
    acc = c0[y]
    for d in range(7):
        acc = acc + ry0[d]
    own0[...] = acc
    gy0[y] = acc
    g0 = [send(own0, gy0.at[y], ypeer(d)) for d in (4, 3, 5, 2, 6, 1, 7)]

    arrive(x1)
    acc = c1[x] + rx1[0] + rx1[1] + rx1[2]
    own1[...] = acc
    gx1[x] = acc
    g1 = [send(own1, gx1.at[x], xpeer(d)) for d in (2, 1, 3)]

    arrive(g0)
    mine0 = pl.ds(pl.multiple_of(x * 144, 8), 144)
    pf_ref[0, mine0] = jnp.concatenate([gy0[yy, 0:18] for yy in range(NY)], axis=0)
    h0 = [send(pf_ref.at[0, mine0], pf_ref.at[0, mine0], xpeer(d)) for d in (2, 1, 3)]

    arrive(g1)
    mine1 = pl.ds(pl.multiple_of(y * 72, 8), 72)
    pf_ref[1, mine1] = jnp.concatenate([gx1[xx, 0:18] for xx in range(NX)], axis=0)
    h1 = [send(pf_ref.at[1, mine1], pf_ref.at[1, mine1], ypeer(d)) for d in (4, 3, 5, 2, 6, 1, 7)]

    arrive(vx)
    vc[...] = vpk[pl.ds(x * NY, NY)] + vrx[0] + vrx[1] + vrx[2]
    vy = []
    for d in (4, 3, 5, 2, 6, 1, 7):
        vy.append(send(vc.at[lax.rem(y + d, NY)], vry.at[d - 1], ypeer(d)))

    def right(s):
        hi, lo = split(pf_ref[s])
        lhs = jnp.concatenate([hi, lo], axis=1)
        total = None
        for j in range(4):
            rows = slice(576 * j, 576 * j + 576)
            term = dot(lhs, jnp.concatenate([gv[s, rows], ev[s, rows]], axis=1), ((0,), (0,)))
            term = term[32 * j:32 * j + 32] + term[128 + 32 * j:160 + 32 * j]
            total = term if total is None else total + term
        total = total[:, :128] + total[:, 128:]
        for i in range(4):
            tt[4 * s + i] = total[8 * i:8 * i + 8]

    arrive(h0)
    right(0)
    arrive(h1)
    right(1)
    ty = []
    for d in (4, 3, 5, 2, 6, 1, 7):
        ty.append(send(tt.at[lax.rem(y + d, NY)], try_.at[d - 1], ypeer(d)))

    gram = None
    for s in range(2):
        p = pf_ref[s]
        wide = jnp.where(row_block == lane_block, dot(p, p, ((0,), (0,)), HIGH), 0.0)
        pick = (lane_k == 32 * s + lax.rem(row_k, 32)).astype(f32)
        term = dot(pick, dot(wide, pick, precision=HIGH), ((0,), (0,)), HIGH)
        gram = term if gram is None else gram + term
    squares = gram * gram
    slot_of = row_k[:, :1] // 32
    sums = jnp.sum(squares, axis=1, keepdims=True)
    scale = [jnp.sqrt(jnp.sum(jnp.where(slot_of == s, sums, 0.0), axis=0, keepdims=True) + 1e-06) for s in range(2)]
    scale_row = jnp.where(slot_of == 0, scale[0], scale[1])
    eye = (row_k == lane_k).astype(f32)
    cur = gram / scale_row
    root = eye
    for step in range(NS_ITERS):
        fm = 1.5 * eye - 0.5 * (cur if step == 0 else dot(root, cur, precision=HIGH))
        if step < NS_ITERS - 1:
            cur = dot(cur, fm, precision=HIGH)
        root = fm if step == 0 else dot(fm, root, precision=HIGH)
    inv_sqrt = 1.0 / jnp.sqrt(scale_row)
    pm = dot(root, dot(gram, root, precision=HIGH), ((0,), (0,)), HIGH) / scale_row

    arrive(vy)
    vsum = vc[y]
    for d in range(7):
        vsum = vsum + vry[d]
    vs_ref[...] = vsum
    vmean = vsum * (1.0 / 32.0)
    vsq = jnp.sum(jnp.sum(vmean * vmean, axis=1, keepdims=True), axis=0, keepdims=True)

    arrive(ty)
    acc = tt[y]
    for d in range(7):
        acc = acc + try_[d]
    tx[x] = jnp.concatenate([acc, jnp.broadcast_to(vsq, (8, 128))], axis=0)
    t2 = [send(tx.at[x], tx.at[x], xpeer(d)) for d in (2, 1, 3)]
    arrive(t2)
    tf[y] = (tx[0] + tx[1]) + (tx[2] + tx[3])
    t3 = [send(tf.at[y], tf.at[y], ypeer(d)) for d in (4, 3, 5, 2, 6, 1, 7)]
    arrive(t3)
    tfull = jnp.concatenate([tf[yy, 0:8] for yy in range(NY)] + [jnp.zeros((64, 128), f32)], axis=0)
    vtot = tf[0, 8:16]
    for yy in range(1, NY):
        vtot = vtot + tf[yy, 8:16]

    count = jnp.int32(0)
    for n in range(own_ref.shape[0]):
        count = count + jnp.where(own_ref[n] == o, 1, 0).astype(jnp.int32)
    live_row = (slot_of < jnp.minimum(count, 2)).astype(f32)

    qt = dot(root, tfull, ((0,), (0,)), HIGH) * (inv_sqrt * (1.0 / 32.0))
    qm = dot(qt, qt, ((1,), (1,)), HIGH)
    part = jnp.sum(jnp.sum(pm * qm, axis=1, keepdims=True) * live_row, axis=0, keepdims=True)
    sc[o] = jnp.broadcast_to(part, (8, 128)) + vtot
    s1 = [send(sc.at[o], sc.at[o], opeer(d)) for d in (8, 7, 9, 6, 10, 5, 11, 4, 12, 3, 13, 2, 14, 1, 15)]
    b_ref[...] = (dot(root, qt, precision=HIGH) * inv_sqrt)[:64]
    qt_ref[...] = qt[:64]
    arrive(s1)
    total_sq = sc[0]
    for n in range(1, NO):
        total_sq = total_sq + sc[n]
    fac_ref[...] = jnp.minimum(1.0, clip_limit / jnp.sqrt(total_sq / entries + 1e-06))
    for copy in started:
        copy.wait_send()


def update_kernel(
    own_ref, fac_ref, pf_ref, b_ref, qt_ref, vs_ref, grad_ref, err_ref, q_ref, w_ref, m_ref, vw_ref, vm_ref,
    wn_ref, mn_ref, en_ref, qn_ref, vwn_ref, vmn_ref,
):
    r = lax.axis_index("replica")
    o = lax.axis_index("owner")
    s = pl.program_id(0)
    count = jnp.int32(0)
    for n in range(own_ref.shape[0]):
        count = count + jnp.where(own_ref[n] == o, 1, 0).astype(jnp.int32)
    live = s < count
    lane_block = lax.broadcasted_iota(jnp.int32, (128, 128), 0) // 32
    b = b_ref[...]
    wide = jnp.concatenate([b] * 4, axis=0)
    hi, lo = split(wide)
    zero = jnp.zeros_like(hi)
    phi, plo = split(pf_ref[...])
    lhs = jnp.concatenate([phi, plo], axis=1)

    def product(lhs, keep):
        bh, bl = jnp.where(keep, hi, zero), jnp.where(keep, lo, zero)
        return dot(lhs, jnp.concatenate([bh, bh], axis=0)) + dot(lhs[:, :128], bl)

    for j in range(4):
        rows = slice(576 * j, 576 * j + 576)
        approx = product(lhs, lane_block == j)
        e = err_ref[0, 0, rows]
        merged = grad_ref[0, 0, rows].astype(f32) + e.astype(f32)
        en_ref[0, 0, rows] = jnp.where(live, (merged - approx).astype(bf16), e)

    fac = fac_ref[0:1, :]
    at = pl.multiple_of(lax.rem(r, 8) * 72, 8)
    rhi, rlo = split(pf_ref[pl.ds(at, 72)])
    rows_lhs = jnp.concatenate([rhi, rlo], axis=1)
    approx = product(rows_lhs, lane_block == r // 8)
    m = m_ref[0]
    mn = jnp.where(live, momentum_decay * m + fac * approx, m)
    mn_ref[0] = mn
    w = w_ref[0]
    wn_ref[0] = jnp.where(live, w - learn_rate * mn, w)
    qn_ref[0] = jnp.where(live, qt_ref[...].T, q_ref[0])
    vmean = vs_ref[:, :72] * (1.0 / 32.0)
    vmn = momentum_decay * vm_ref[...] + fac[:, :72] * vmean
    vmn_ref[...] = vmn
    vwn_ref[...] = vw_ref[...] - learn_rate * vmn


def on_device(owner_of, grad, error, q_prev, weight, momentum, vec_grad, vec_weight, vec_mom):
    S = jax.ShapeDtypeStruct
    vm = pl.BlockSpec(memory_space=pltpu.VMEM)
    hbm = pl.BlockSpec(memory_space=pl.ANY)
    smem = pl.BlockSpec(memory_space=pltpu.SMEM)
    width = grad.shape[2]
    entries = float(owner_of.shape[0] * width * grad.shape[3] + NO * vec_grad.shape[1] * width)
    n_sends = 3 + 7 + 7 + 3 + 3 + 7 + 3 + 3 + 7 + 7 + 7 + 3 + 7 + 15
    V = pltpu.VMEM
    pf, b, qt, vs, fac = pl.pallas_call(
        functools.partial(gather_kernel, entries=entries),
        out_shape=(S((2, 576, 128), f32), S((64, 128), f32), S((64, 128), f32), S((8, 128), f32), S((8, 128), f32)),
        in_specs=[smem, hbm, hbm, hbm, hbm],
        out_specs=(vm, vm, vm, vm, vm),
        scratch_shapes=[
            V((2, 2304, 128), bf16), V((2, 2304, 128), bf16), V((2, 128, 32), f32), V((8, 2304), bf16),
            V((2, 576, 128), f32),
            V((3, 144, 128), f32), V((8, 24, 128), f32), V((7, 24, 128), f32), V((24, 128), f32), V((8, 24, 128), f32),
            V((7, 72, 128), f32), V((4, 24, 128), f32), V((3, 24, 128), f32), V((24, 128), f32), V((4, 24, 128), f32),
            V((32, 8, 128), f32), V((3, 8, 8, 128), f32), V((8, 8, 128), f32), V((7, 8, 128), f32),
            V((8, 8, 128), f32), V((7, 8, 128), f32), V((4, 16, 128), f32), V((8, 16, 128), f32), V((16, 8, 128), f32),
            pltpu.SemaphoreType.DMA((6,)),
            pltpu.SemaphoreType.DMA((n_sends,)),
            pltpu.SemaphoreType.DMA((n_sends,)),
        ],
        compiler_params=pltpu.CompilerParams(collective_id=0, has_side_effects=True),
        name="gather",
    )(owner_of, grad, error, q_prev, vec_grad)

    full = lambda shape: pl.BlockSpec(shape, lambda s: (0,) * len(shape))
    slot = lambda shape: pl.BlockSpec((1,) + shape, lambda s: (s,) + (0,) * len(shape))
    big = pl.BlockSpec((1, 1, 2304, 128), lambda s: (0, s, 0, 0))
    half = pl.BlockSpec((32, 128), lambda s: (s, 0))
    return pl.pallas_call(
        update_kernel,
        grid=(2,),
        out_shape=(
            S(weight.shape, f32), S(momentum.shape, f32), S(error.shape, bf16), S(q_prev.shape, f32),
            S(vec_weight.shape, f32), S(vec_mom.shape, f32),
        ),
        in_specs=[
            smem, full((8, 128)), pl.BlockSpec((None, 576, 128), lambda s: (s, 0, 0)), half, half, full((8, 128)),
            big, big, slot((128, 32)), slot((72, 128)), slot((72, 128)), full((8, 72)), full((8, 72)),
        ],
        out_specs=(
            slot((72, 128)), slot((72, 128)), big, slot((128, 32)), full((8, 72)), full((8, 72)),
        ),
        name="update",
    )(owner_of, fac, pf, b, qt, vs, grad, error, q_prev, weight, momentum, vec_weight, vec_mom)


def solution(mesh):
    return jax.shard_map(
        on_device,
        mesh=mesh,
        in_specs=(
            P(),
            P("replica", "owner", None, None),
            P("replica", "owner", None, None),
            P("owner", None, None),
            P("owner", "replica", None),
            P("owner", "replica", None),
            P("replica", "owner", None),
            P("owner", "replica"),
            P("owner", "replica"),
        ),
        out_specs=(
            P("owner", "replica", None),
            P("owner", "replica", None),
            P("replica", "owner", None, None),
            P("owner", None, None),
            P("owner", "replica"),
            P("owner", "replica"),
        ),
        check_vma=False,
    )
```

time: 373 us -> 69.9 us (0.19)
  blocking collectives: 170 us -> 0 us
  waiting for transfers between devices: 159 us -> 0 us
  Pallas kernels: 0 us -> 65.9 us
  matrix products: 17.9 us -> 0 us
  between operations: 16.3 us -> 0.64 us
  other arithmetic: 9.55 us -> 0 us
    psum x2 -> x0, blocking collectives: 170 us -> none  [the longest x1 114 us: on_device(): q_new = lax.psum(right_terms, 'replica') / replicas]
    psum x1 -> x0, waiting for transfers between devices: 159 us -> none  [on_device(): p_sum, vec_sum = lax.psum((left_terms, vec_terms), 'replica')]
    pallas_call x0 -> x2, Pallas kernels: none -> 65.9 us  [the longest x1 62.1 us: on_device(): pl.pallas_call(functools.partial(gather_kernel, entries=entries), out_sha...]
    dot_general x19 -> x0, matrix products: 17.9 us -> none  [the longest x1 5.88 us: on_device(): approx = jnp.einsum('sdk,swk->sdw', p_hat, q_new, precision=exact_mode)]
  transfers between devices with their start and end apart: 1 -> 0, of which waited for: 1 -> 0; matrix products, arithmetic and copies ran while one was open for 0% -> 0% of each run, Pallas kernels for 0% -> 0%
where the time goes in v1:
time: 69.9 us; the launch traced here: 69.6 us
  Pallas kernels  65.9 us (94%)
  local copies, waits for them, and re-layouts  3.1 us (4%)
    pallas_call x1, Pallas kernels, on_device(): pl.pallas_call(functools.partial(gather_kernel, entries=entries), out_sha...  62.1 us
    pallas_call x1, Pallas kernels, on_device(): pl.pallas_call(update_kernel, grid=(2,), out_shape=(S(weight.shape, f32),...  3.72 us
    pallas_call x1, local copies, waits for them, and re-layouts, on_device(): pl.pallas_call(update_kernel, grid=(2,), out_shape=(S(weight.shape, f32),...  1.59 us
    unnamed x1, local copies, waits for them, and re-layouts  1.5 us

profile of v1, /device:TPU:1, one launch (start us, length us, event | category | flops | bytes accessed | tf_op | source)
XLA Modules:
  0.0 69.6 jit_solution(14193905738034229108)
XLA Ops:
  0.6 1.5 %copy.15.q_ref = f32[2,128,32]{2,1,0:T(8,128)} copy(f32[2,128,32]{1,2,0:T(8,128)} %param.12) | data formatting | bytes 65536 | tf_op args[3]
  2.1 62.1 %gather.1 = (f32[2,576,128]{2,1,0:T(8,128)}, f32[64,128]{1,0:T(8,128)}, f32[64,128]{1,0:T(8,128)}, f32[8,128]{1,0:T(8,128)}, f32[8,128]{1,0:T(8,128)}) custom-call(s32[24]{0:T(128)} %own_ref.3, bf16[1,2,2304,128]{3,2,1,0:T(8,128)(2,1)} %grad_ref.3, bf16[1,2,2304,128]{3,2,1,0:T(8,128)(2,1)} %err_ref.3, f32[2,128,32]{2,1,0:T(8,128)} %copy.15.q_ref, ...), custom_call_target="tpu_custom_call" | custom-call | tf_op jit(solution)/shard_map/gather/pallas_call | solution.py:323
  64.3 3.7 %update.1 = (f32[2,72,128]{2,1,0:T(8,128)}, f32[2,72,128]{2,1,0:T(8,128)}, bf16[1,2,2304,128]{3,2,1,0:T(8,128)(2,1)}, f32[2,128,32]{2,1,0:T(8,128)}, f32[8,72]{1,0:T(8,128)}, /*index=5*/f32[8,72]{1,0:T(8,128)}) custom-call(s32[24]{0:T(128)} %own_ref.3, f32[8,128]{1,0:T(8,128)} %get-tuple-element.11.fac_ref, f32[2,576,128]{2,1,0:T(8,128)} %get-tuple-element.12.pf_ref, ...), custom_call_target="tpu_custom_call" | custom-call | tf_op jit(solution)/shard_map/update/pallas_call | solution.py:347
  68.0 1.6 %copy.17 = f32[2,128,32]{1,2,0:T(8,128)} copy(f32[2,128,32]{2,1,0:T(8,128)} %get-tuple-element.19) | data formatting | bytes 65536 | tf_op jit(solution)/shard_map/update/pallas_call | solution.py:347

commit v2 on v1

--- a/solution.py
+++ b/solution.py
@@ -83,7 +83,7 @@
     row_k = lax.broadcasted_iota(jnp.int32, (128, 128), 0)
 
     def left(s):
-        wide = jnp.concatenate([qv[s]] * 4, axis=1)
+        wide = jnp.concatenate([qv[s]] * 4, axis=0).T
         hi, lo = split(wide)
         total = None
         for j in range(4):
@@ -304,7 +304,7 @@
     mn_ref[0] = mn
     w = w_ref[0]
     wn_ref[0] = jnp.where(live, w - learn_rate * mn, w)
-    qn_ref[0] = jnp.where(live, qt_ref[...].T, q_ref[0])
+    qn_ref[0] = jnp.where(live, qt_ref[...], q_ref[0])
     vmean = vs_ref[:, :72] * (1.0 / 32.0)
     vmn = momentum_decay * vm_ref[...] + fac[:, :72] * vmean
     vmn_ref[...] = vmn
@@ -320,13 +320,14 @@
     entries = float(owner_of.shape[0] * width * grad.shape[3] + NO * vec_grad.shape[1] * width)
     n_sends = 3 + 7 + 7 + 3 + 3 + 7 + 3 + 3 + 7 + 7 + 7 + 3 + 7 + 15
     V = pltpu.VMEM
+    q_rows = jnp.swapaxes(q_prev, 1, 2)
     pf, b, qt, vs, fac = pl.pallas_call(
         functools.partial(gather_kernel, entries=entries),
         out_shape=(S((2, 576, 128), f32), S((64, 128), f32), S((64, 128), f32), S((8, 128), f32), S((8, 128), f32)),
         in_specs=[smem, hbm, hbm, hbm, hbm],
         out_specs=(vm, vm, vm, vm, vm),
         scratch_shapes=[
-            V((2, 2304, 128), bf16), V((2, 2304, 128), bf16), V((2, 128, 32), f32), V((8, 2304), bf16),
+            V((2, 2304, 128), bf16), V((2, 2304, 128), bf16), V((2, 32, 128), f32), V((8, 2304), bf16),
             V((2, 576, 128), f32),
             V((3, 144, 128), f32), V((8, 24, 128), f32), V((7, 24, 128), f32), V((24, 128), f32), V((8, 24, 128), f32),
             V((7, 72, 128), f32), V((4, 24, 128), f32), V((3, 24, 128), f32), V((24, 128), f32), V((4, 24, 128), f32),
@@ -338,28 +339,29 @@
         ],
         compiler_params=pltpu.CompilerParams(collective_id=0, has_side_effects=True),
         name="gather",
-    )(owner_of, grad, error, q_prev, vec_grad)
+    )(owner_of, grad, error, q_rows, vec_grad)
 
     full = lambda shape: pl.BlockSpec(shape, lambda s: (0,) * len(shape))
     slot = lambda shape: pl.BlockSpec((1,) + shape, lambda s: (s,) + (0,) * len(shape))
     big = pl.BlockSpec((1, 1, 2304, 128), lambda s: (0, s, 0, 0))
     half = pl.BlockSpec((32, 128), lambda s: (s, 0))
-    return pl.pallas_call(
+    wn, mn, en, qn, vwn, vmn = pl.pallas_call(
         update_kernel,
         grid=(2,),
         out_shape=(
-            S(weight.shape, f32), S(momentum.shape, f32), S(error.shape, bf16), S(q_prev.shape, f32),
+            S(weight.shape, f32), S(momentum.shape, f32), S(error.shape, bf16), S(q_rows.shape, f32),
             S(vec_weight.shape, f32), S(vec_mom.shape, f32),
         ),
         in_specs=[
             smem, full((8, 128)), pl.BlockSpec((None, 576, 128), lambda s: (s, 0, 0)), half, half, full((8, 128)),
-            big, big, slot((128, 32)), slot((72, 128)), slot((72, 128)), full((8, 72)), full((8, 72)),
+            big, big, slot((32, 128)), slot((72, 128)), slot((72, 128)), full((8, 72)), full((8, 72)),
         ],
         out_specs=(
-            slot((72, 128)), slot((72, 128)), big, slot((128, 32)), full((8, 72)), full((8, 72)),
+            slot((72, 128)), slot((72, 128)), big, slot((32, 128)), full((8, 72)), full((8, 72)),
         ),
         name="update",
-    )(owner_of, fac, pf, b, qt, vs, grad, error, q_prev, weight, momentum, vec_weight, vec_mom)
+    )(owner_of, fac, pf, b, qt, vs, grad, error, q_rows, weight, momentum, vec_weight, vec_mom)
+    return wn, mn, en, jnp.swapaxes(qn, 1, 2), vwn, vmn
 
 
 def solution(mesh):

time: 69.9 us -> 66.6 us (0.953)
  local copies, waits for them, and re-layouts: 3.1 us -> 0 us
    pallas_call x1 -> x0, local copies, waits for them, and re-layouts: 1.59 us -> none  [on_device(): pl.pallas_call(update_kernel, grid=(2,), out_shape=(S(weight.shape, f32),...]
    unnamed x1 -> x0, local copies, waits for them, and re-layouts: 1.5 us -> none
where the time goes in v2:
time: 66.6 us; the launch traced here: 66.5 us
  Pallas kernels  65.8 us (99%)
    pallas_call x1, Pallas kernels, on_device(): pl.pallas_call(functools.partial(gather_kernel, entries=entries), out_sha...  62.1 us
    pallas_call x1, Pallas kernels, on_device(): pl.pallas_call(update_kernel, grid=(2,), out_shape=(S(weight.shape, f32),...  3.69 us

profile of v2, /device:TPU:1, one launch (start us, length us, event | category | flops | bytes accessed | tf_op | source)
XLA Modules:
  0.0 66.5 jit_solution(2587508071870026226)
XLA Ops:
  0.6 62.1 %gather.1 = (f32[2,576,128]{2,1,0:T(8,128)}, f32[64,128]{1,0:T(8,128)}, f32[64,128]{1,0:T(8,128)}, f32[8,128]{1,0:T(8,128)}, f32[8,128]{1,0:T(8,128)}) custom-call(s32[24]{0:T(128)} %own_ref.3, bf16[1,2,2304,128]{3,2,1,0:T(8,128)(2,1)} %grad_ref.3, bf16[1,2,2304,128]{3,2,1,0:T(8,128)(2,1)} %err_ref.3, f32[2,32,128]{2,1,0:T(8,128)} %bitcast.2, ...), custom_call_target="tpu_custom_call" | custom-call | tf_op jit(solution)/shard_map/gather/pallas_call | solution.py:324
  62.8 3.7 %update.1 = (f32[2,72,128]{2,1,0:T(8,128)}, f32[2,72,128]{2,1,0:T(8,128)}, bf16[1,2,2304,128]{3,2,1,0:T(8,128)(2,1)}, f32[2,32,128]{2,1,0:T(8,128)}, f32[8,72]{1,0:T(8,128)}, /*index=5*/f32[8,72]{1,0:T(8,128)}) custom-call(s32[24]{0:T(128)} %own_ref.3, f32[8,128]{1,0:T(8,128)} %get-tuple-element.17.fac_ref, f32[2,576,128]{2,1,0:T(8,128)} %get-tuple-element.18.pf_ref, ...), custom_call_target="tpu_custom_call" | custom-call | tf_op jit(solution)/shard_map/update/pallas_call | solution.py:348

commit v3 on v0

v3 whole, which is shorter than its diff:
```python
import functools

import jax
import jax.numpy as jnp
from jax import lax
from jax.experimental import pallas as pl
from jax.experimental.pallas import tpu as pltpu
from jax.sharding import PartitionSpec as P

MESH = pl.DeviceIdType.MESH
NS_ITERS = 5
NX, NY, NO = 4, 8, 16
clip_limit = 0.1
momentum_decay = 0.9
learn_rate = 0.05
f32, bf16 = jnp.float32, jnp.bfloat16
HIGH = lax.Precision.HIGHEST
XFAR = (2, 1, 3)
YFAR = (4, 3, 5, 2, 6, 1, 7)
OFAR = (8, 7, 9, 6, 10, 5, 11, 4, 12, 3, 13, 2, 14, 1, 15)


def split(a):
    hi = a.astype(bf16)
    return hi, (a - hi.astype(f32)).astype(bf16)


def dot(a, b, dims=((1,), (0,)), precision=None):
    return lax.dot_general(a, b, (dims, ((), ())), precision=precision, preferred_element_type=f32)


def step_kernel(
    own_ref, grad_ref, err_ref, q_ref, vec_ref, w_ref, m_ref, vw_ref, vm_ref,
    wn_ref, mn_ref, en_ref, qn_ref, vwn_ref, vmn_ref,
    gv, ev, qv, vv, wv, mv, vwv, vmv, loc, pf, rx0, a0, ry0, ry1, c1, rx1, own1, gx1,
    vpk, vrx, vc, vry, vqy, vqx, tt, try_, tx, tf, sc,
    load_sem, send_sem, recv_sem,
    *, entries,
):
    r = lax.axis_index("replica")
    o = lax.axis_index("owner")
    x, y = lax.rem(r, NX), r // NX

    def xpeer(d):
        return (y * NX + lax.rem(x + d, NX), o)

    def ypeer(d):
        return (lax.rem(y + d, NY) * NX + x, o)

    def opeer(d):
        return (r, lax.rem(o + d, NO))

    barrier = pltpu.get_barrier_semaphore()
    peers = [ypeer(d) for d in YFAR] + [opeer(d) for d in OFAR] + [xpeer(d) for d in XFAR]
    for peer in peers:
        pl.semaphore_signal(barrier, inc=1, device_id=peer, device_id_type=MESH)

    loads = []
    for n, (src, dst) in enumerate(
        [(q_ref, qv), (grad_ref.at[0, 0], gv.at[0]), (err_ref.at[0, 0], ev.at[0]),
         (grad_ref.at[0, 1], gv.at[1]), (err_ref.at[0, 1], ev.at[1]), (vec_ref.at[0], vv),
         (w_ref, wv), (m_ref, mv), (vw_ref, vwv), (vm_ref, vmv)]
    ):
        copy = pltpu.make_async_copy(src, dst, load_sem.at[n])
        copy.start()
        loads.append(copy)

    started = []

    def send(src, dst, peer):
        n = len(started)
        copy = pltpu.make_async_remote_copy(
            src_ref=src, dst_ref=dst, send_sem=send_sem.at[n], recv_sem=recv_sem.at[n],
            device_id=peer, device_id_type=MESH,
        )
        copy.start()
        started.append(copy)
        return copy

    def arrive(copies):
        for copy in copies:
            copy.wait_recv()

    def rows(start, size):
        return pl.ds(pl.multiple_of(start, 8), size)

    lane_k = lax.broadcasted_iota(jnp.int32, (128, 128), 1)
    row_k = lax.broadcasted_iota(jnp.int32, (128, 128), 0)
    lane_block, row_block = lane_k // 32, row_k // 32

    def left(s):
        wide = jnp.concatenate([qv[s]] * 4, axis=0).T
        hi, lo = split(wide)
        zero = jnp.zeros_like(hi)
        total = None
        for j in range(4):
            keep = lane_block == j
            half = jnp.concatenate([jnp.where(keep, hi, zero), jnp.where(keep, lo, zero)], axis=1)
            rhs = jnp.concatenate([half, half], axis=0)
            part = slice(576 * j, 576 * j + 576)
            term = dot(jnp.concatenate([gv[s, part], ev[s, part]], axis=1), rhs)
            total = term if total is None else total + term
        loc[576 * s:576 * s + 576] = total[:, :128] + total[:, 128:]

    loads[0].wait()
    loads[3].wait()
    loads[4].wait()
    left(1)
    loads[1].wait()
    loads[2].wait()
    left(0)
    pl.semaphore_wait(barrier, len(peers))

    x0, y1 = [], []
    for n in range(7):
        to = lax.rem(y + YFAR[n], NY)
        y1.append(send(loc.at[rows(768 + to * 48, 48)], ry1.at[YFAR[n] - 1], ypeer(YFAR[n])))
        if n < 3:
            to = lax.rem(x + XFAR[n], NX)
            x0.append(send(loc.at[rows(to * 192, 192)], rx0.at[XFAR[n] - 1], xpeer(XFAR[n])))

    for load in loads[5:]:
        load.wait()
    vall = vv[...].astype(f32)
    for yy in range(NY):
        for xx in range(NX):
            at = 72 * (NX * yy + xx)
            vpk[xx * NY + yy] = jnp.concatenate([vall[:, at:at + 72], jnp.zeros((8, 56), f32)], axis=1)

    arrive(x0)
    a0[...] = loc[rows(x * 192, 192)] + rx0[0] + rx0[1] + rx0[2]
    y0 = [send(a0.at[rows(lax.rem(y + d, NY) * 24, 24)], ry0.at[d - 1], ypeer(d)) for d in YFAR]

    arrive(y1)
    acc = loc[rows(768 + y * 48, 48)]
    for d in range(7):
        acc = acc + ry1[d]
    pad4 = jnp.zeros((4, 128), f32)
    for xx in range(NX):
        c1[xx] = jnp.concatenate([acc[12 * xx:12 * xx + 12], pad4], axis=0)
    x1 = [send(c1.at[lax.rem(x + d, NX)], rx1.at[d - 1], xpeer(d)) for d in XFAR]
    vx = [send(vpk.at[pl.ds(lax.rem(x + d, NX) * NY, NY)], vrx.at[d - 1], xpeer(d)) for d in XFAR]

    arrive(x1)
    acc = c1[x] + rx1[0] + rx1[1] + rx1[2]
    own1[...] = acc
    gx1[x] = acc
    g1 = [send(own1, gx1.at[x], xpeer(d)) for d in XFAR]

    arrive(y0)
    acc = a0[rows(y * 24, 24)]
    for d in range(7):
        acc = acc + ry0[d]
    mine = rows(x * 192 + y * 24, 24)
    pf[mine] = acc
    g0 = [send(pf.at[mine], pf.at[mine], ypeer(d)) for d in YFAR]

    arrive(g1)
    block1 = rows(768 + y * 48, 48)
    pf[block1] = jnp.concatenate([gx1[xx, 0:12] for xx in range(NX)], axis=0)
    h1 = [send(pf.at[block1], pf.at[block1], ypeer(d)) for d in YFAR]

    arrive(vx)
    vc[...] = vpk[pl.ds(x * NY, NY)] + vrx[0] + vrx[1] + vrx[2]
    vy = [send(vc.at[lax.rem(y + d, NY)], vry.at[d - 1], ypeer(d)) for d in YFAR]

    arrive(g0)
    block0 = rows(x * 192, 192)
    h0 = [send(pf.at[block0], pf.at[block0], xpeer(d)) for d in XFAR]

    arrive(vy)
    vsum = vc[y]
    for d in range(7):
        vsum = vsum + vry[d]
    vmean = vsum * (1.0 / 32.0)
    vqy[y] = jnp.sum(vmean * vmean, axis=0, keepdims=True)

    def right(s):
        hi, lo = split(pf[576 * s:576 * s + 576])
        lhs = jnp.concatenate([hi, lo], axis=1)
        total = None
        for j in range(4):
            part = slice(576 * j, 576 * j + 576)
            term = dot(lhs, jnp.concatenate([gv[s, part], ev[s, part]], axis=1), ((0,), (0,)))
            term = term[32 * j:32 * j + 32] + term[128 + 32 * j:160 + 32 * j]
            total = term if total is None else total + term
        total = total[:, :128] + total[:, 128:]
        for i in range(4):
            tt[4 * s + i] = total[8 * i:8 * i + 8]

    arrive(h0)
    right(0)
    arrive(h1)
    right(1)
    ty = [send(tt.at[lax.rem(y + d, NY)], try_.at[d - 1], ypeer(d)) for d in YFAR]
    qy = [send(vqy.at[y], vqy.at[y], ypeer(d)) for d in YFAR]

    def pad(a):
        return jnp.concatenate([a, jnp.zeros((64, 128), f32)], axis=0)

    grams = []
    for s in range(2):
        p = pf[576 * s:576 * s + 576]
        wide = jnp.where(row_block == lane_block, dot(p, p, ((0,), (0,)), HIGH), 0.0)
        g = (wide[0:32] + wide[32:64]) + (wide[64:96] + wide[96:128])
        g = g + pltpu.roll(g, 64, 1)
        g = g + pltpu.roll(g, 32, 1)
        grams.append(jnp.where(lane_block[:32] == s, g, 0.0))
    gram = jnp.concatenate(grams, axis=0)
    scale = [
        jnp.sqrt(jnp.sum(jnp.sum(g * g, axis=0, keepdims=True), axis=1, keepdims=True) + 1e-06) for g in grams
    ]
    slot_of = row_k[:64, :1] // 32
    scale_row = jnp.where(slot_of == 0, scale[0], scale[1])
    eye = (row_k == lane_k).astype(f32)[:64]
    cur = gram / scale_row
    root = eye
    for step in range(NS_ITERS):
        fm = 1.5 * eye - 0.5 * (cur if step == 0 else dot(root, pad(cur), precision=HIGH))
        if step < NS_ITERS - 1:
            cur = dot(cur, pad(fm), precision=HIGH)
        root = fm if step == 0 else dot(fm, pad(root), precision=HIGH)

    arrive(ty)
    acc = tt[y]
    for d in range(7):
        acc = acc + try_[d]
    tx[x] = acc
    t2 = [send(tx.at[x], tx.at[x], xpeer(d)) for d in XFAR]
    arrive(qy)
    acc = vqy[0]
    for yy in range(1, NY):
        acc = acc + vqy[yy]
    vqx[x] = acc
    qx = [send(vqx.at[x], vqx.at[x], xpeer(d)) for d in XFAR]

    inv_sqrt = 1.0 / jnp.sqrt(scale_row)
    root_t = pad(root).T[:64]
    qm = root_t * (inv_sqrt * (1.0 / 32.0))
    bm = dot(root * inv_sqrt, pad(qm), precision=HIGH)

    arrive(t2)
    tf[y] = (tx[0] + tx[1]) + (tx[2] + tx[3])
    t3 = [send(tf.at[y], tf.at[y], ypeer(d)) for d in YFAR]

    pm = dot(root_t, pad(dot(gram, pad(root), precision=HIGH)), precision=HIGH) / scale_row
    pm = dot(pm, pad(qm), precision=HIGH)
    lhs = jnp.concatenate([qm, pm, bm], axis=0)
    arrive(qx)
    vtot = (vqx[0] + vqx[1]) + (vqx[2] + vqx[3])
    count = jnp.int32(0)
    for n in range(own_ref.shape[0]):
        count = count + jnp.where(own_ref[n] == o, 1, 0).astype(jnp.int32)
    live_row = (slot_of < count).astype(f32)

    arrive(t3)
    tfull = jnp.concatenate([tf[yy] for yy in range(NY)], axis=0)
    out = dot(lhs, pad(tfull), precision=HIGH)
    qt, pq, b = out[0:64], out[64:128], out[128:192]
    sc[o] = jnp.sum(qt * pq * live_row, axis=0, keepdims=True) + vtot
    s1 = [send(sc.at[o], sc.at[o], opeer(d)) for d in OFAR]

    approx_rows = []
    for s in range(2):
        live = s < count
        hi, lo = split(jnp.concatenate([b[32 * s:32 * s + 32]] * 4, axis=0))
        zero = jnp.zeros_like(hi)

        def product(p, keep):
            phi, plo = split(p)
            bh, bl = jnp.where(keep, hi, zero), jnp.where(keep, lo, zero)
            return dot(jnp.concatenate([phi, plo], axis=1), jnp.concatenate([bh, bh], axis=0)) + dot(phi, bl)

        for j in range(4):
            part = slice(576 * j, 576 * j + 576)
            approx = product(pf[576 * s:576 * s + 576], row_block == j)
            e = ev[s, part]
            merged = gv[s, part].astype(f32) + e.astype(f32)
            en_ref[0, s, part] = jnp.where(live, (merged - approx).astype(bf16), e)
        approx_rows.append(product(pf[rows(576 * s + lax.rem(r, 8) * 72, 72)], row_block == r // 8))
        qn_ref[s] = jnp.where(live, qt[32 * s:32 * s + 32], qv[s])

    arrive(s1)
    total = sc[0]
    for n in range(1, NO):
        total = total + sc[n]
    total_sq = jnp.sum(total, axis=1, keepdims=True)
    fac = jnp.minimum(1.0, clip_limit / jnp.sqrt(total_sq / entries + 1e-06))
    for s in range(2):
        live = s < count
        m = mv[s]
        mn = jnp.where(live, momentum_decay * m + fac * approx_rows[s], m)
        mn_ref[s] = mn
        wn_ref[s] = jnp.where(live, wv[s] - learn_rate * mn, wv[s])
    vmn = momentum_decay * vmv[...] + fac * vmean[:, :72]
    vmn_ref[...] = vmn
    vwn_ref[...] = vwv[...] - learn_rate * vmn
    for copy in started:
        copy.wait_send()


def move_kernel(*refs):
    n = len(refs) // 2
    copies = [pltpu.make_async_copy(refs[i], refs[n + i], refs[2 * n].at[i]) for i in (2, 0, 1, 3, 4, 5)]
    for copy in copies:
        copy.start()
    for copy in copies:
        copy.wait()


def on_device(owner_of, grad, error, q_prev, weight, momentum, vec_grad, vec_weight, vec_mom):
    S = jax.ShapeDtypeStruct
    vm = pl.BlockSpec(memory_space=pltpu.VMEM)
    hbm = pl.BlockSpec(memory_space=pltpu.HBM)
    smem = pl.BlockSpec(memory_space=pltpu.SMEM)
    width = grad.shape[2]
    entries = float(owner_of.shape[0] * width * grad.shape[3] + NO * vec_grad.shape[1] * width)
    n_sends = 3 + 7 + 7 + 3 + 3 + 3 + 7 + 7 + 7 + 3 + 7 + 7 + 3 + 3 + 7 + 15
    V = pltpu.VMEM
    q_rows = jnp.swapaxes(q_prev, 1, 2)
    shapes = (
        S(weight.shape, f32), S(momentum.shape, f32), S(error.shape, bf16), S(q_rows.shape, f32),
        S(vec_weight.shape, f32), S(vec_mom.shape, f32),
    )
    results = pl.pallas_call(
        functools.partial(step_kernel, entries=entries),
        out_shape=shapes,
        in_specs=[smem] + [hbm] * 8,
        out_specs=(vm,) * 6,
        scratch_shapes=[
            V((2, 2304, 128), bf16), V((2, 2304, 128), bf16), V((2, 32, 128), f32), V((8, 2304), bf16),
            V((2, 72, 128), f32), V((2, 72, 128), f32), V((8, 72), f32), V((8, 72), f32),
            V((1152, 128), f32), V((1152, 128), f32),
            V((3, 192, 128), f32), V((192, 128), f32), V((7, 24, 128), f32),
            V((7, 48, 128), f32), V((4, 16, 128), f32), V((3, 16, 128), f32), V((16, 128), f32), V((4, 16, 128), f32),
            V((32, 8, 128), f32), V((3, 8, 8, 128), f32), V((8, 8, 128), f32), V((7, 8, 128), f32),
            V((8, 1, 128), f32), V((4, 1, 128), f32),
            V((8, 8, 128), f32), V((7, 8, 128), f32), V((4, 8, 128), f32), V((8, 8, 128), f32), V((16, 1, 128), f32),
            pltpu.SemaphoreType.DMA((10,)),
            pltpu.SemaphoreType.DMA((n_sends,)),
            pltpu.SemaphoreType.DMA((n_sends,)),
        ],
        compiler_params=pltpu.CompilerParams(collective_id=0, has_side_effects=True, vmem_limit_bytes=24 << 20),
        name="step",
    )(owner_of, grad, error, q_rows, vec_grad, weight, momentum, vec_weight, vec_mom)
    wn, mn, en, qn, vwn, vmn = pl.pallas_call(
        move_kernel,
        out_shape=shapes,
        in_specs=[vm] * 6,
        out_specs=(hbm,) * 6,
        scratch_shapes=[pltpu.SemaphoreType.DMA((6,))],
        compiler_params=pltpu.CompilerParams(vmem_limit_bytes=8 << 20),
        name="move",
    )(*results)
    return wn, mn, en, jnp.swapaxes(qn, 1, 2), vwn, vmn


def solution(mesh):
    return jax.shard_map(
        on_device,
        mesh=mesh,
        in_specs=(
            P(),
            P("replica", "owner", None, None),
            P("replica", "owner", None, None),
            P("owner", None, None),
            P("owner", "replica", None),
            P("owner", "replica", None),
            P("replica", "owner", None),
            P("owner", "replica"),
            P("owner", "replica"),
        ),
        out_specs=(
            P("owner", "replica", None),
            P("owner", "replica", None),
            P("replica", "owner", None, None),
            P("owner", None, None),
            P("owner", "replica"),
            P("owner", "replica"),
        ),
        check_vma=False,
    )
```

time: 373 us -> 68.5 us (0.18)
  blocking collectives: 170 us -> 0 us
  waiting for transfers between devices: 159 us -> 0 us
  Pallas kernels: 0 us -> 59.5 us
  matrix products: 17.9 us -> 0 us
  between operations: 16.3 us -> 0.66 us
  other arithmetic: 9.55 us -> 0 us
  local copies, waits for them, and re-layouts: 0.05 us -> 7.85 us
    psum x2 -> x0, blocking collectives: 170 us -> none  [the longest x1 114 us: on_device(): q_new = lax.psum(right_terms, 'replica') / replicas]
    psum x1 -> x0, waiting for transfers between devices: 159 us -> none  [on_device(): p_sum, vec_sum = lax.psum((left_terms, vec_terms), 'replica')]
    pallas_call x0 -> x2, Pallas kernels: none -> 59.5 us  [the longest x1 58.4 us: on_device(): pl.pallas_call(functools.partial(step_kernel, entries=entries), out_shape...]
    dot_general x19 -> x0, matrix products: 17.9 us -> none  [the longest x1 5.88 us: on_device(): approx = jnp.einsum('sdk,swk->sdw', p_hat, q_new, precision=exact_mode)]
    unnamed x20 -> x18, local copies, waits for them, and re-layouts: 0.05 us -> 7.85 us
  transfers between devices with their start and end apart: 1 -> 0, of which waited for: 1 -> 0; matrix products, arithmetic and copies ran while one was open for 0% -> 0% of each run, Pallas kernels for 0% -> 0%
where the time goes in v3:
time: 68.5 us; the launch traced here: 68 us
  Pallas kernels  59.5 us (87%)
  local copies, waits for them, and re-layouts  7.85 us (11%)
    pallas_call x1, Pallas kernels, on_device(): pl.pallas_call(functools.partial(step_kernel, entries=entries), out_shape...  58.4 us
    unnamed x18, local copies, waits for them, and re-layouts  7.85 us

profile of v3, /device:TPU:1, one launch (start us, length us, event | category | flops | bytes accessed | tf_op | source)
XLA Modules:
  0.0 68.0 jit_solution(17034932817584444796)
XLA Ops:
  0.6 0.0 copy-start
  0.6 1.3 %copy-done = bf16[1,2,2304,128]{3,2,1,0:T(8,128)(2,1)S(1)} copy-done((bf16[1,2,2304,128]{3,2,1,0:T(8,128)(2,1)S(1)}, bf16[1,2,2304,128]{3,2,1,0:T(8,128)(2,1)}, u32[]{:S(2)}) %copy-start) | copy-done | bytes 1179672
  1.9 0.0 copy-start.1
  1.9 1.3 %copy-done.1 = bf16[1,2,2304,128]{3,2,1,0:T(8,128)(2,1)S(1)} copy-done((bf16[1,2,2304,128]{3,2,1,0:T(8,128)(2,1)S(1)}, bf16[1,2,2304,128]{3,2,1,0:T(8,128)(2,1)}, u32[]{:S(2)}) %copy-start.1) | copy-done | bytes 1179672
  3.2 0.0 copy-start.2
  3.2 0.9 %copy-done.2 = f32[2,72,128]{2,1,0:T(8,128)S(1)} copy-done((f32[2,72,128]{2,1,0:T(8,128)S(1)}, f32[2,72,128]{2,1,0:T(8,128)}, u32[]{:S(2)}) %copy-start.2) | copy-done | bytes 73752
  4.1 0.0 copy-start.3
  4.1 0.9 %copy-done.3 = f32[2,72,128]{2,1,0:T(8,128)S(1)} copy-done((f32[2,72,128]{2,1,0:T(8,128)S(1)}, f32[2,72,128]{2,1,0:T(8,128)}, u32[]{:S(2)}) %copy-start.3) | copy-done | bytes 73752
  4.9 0.0 copy-start.4
  4.9 0.8 %copy-done.4 = bf16[1,8,2304]{2,1,0:T(8,128)(2,1)S(1)} copy-done((bf16[1,8,2304]{2,1,0:T(8,128)(2,1)S(1)}, bf16[1,8,2304]{2,1,0:T(8,128)(2,1)}, u32[]{:S(2)}) %copy-start.4) | copy-done | bytes 36888
  5.7 0.0 copy-start.5
  5.7 0.8 %copy-done.5 = f32[2,128,32]{1,2,0:T(8,128)S(1)} copy-done((f32[2,128,32]{1,2,0:T(8,128)S(1)}, f32[2,128,32]{1,2,0:T(8,128)}, u32[]{:S(2)}) %copy-start.5) | copy-done | bytes 32792
  6.5 0.0 copy-start.6
  6.5 0.7 %copy-done.6 = f32[8,72]{1,0:T(8,128)S(1)} copy-done((f32[8,72]{1,0:T(8,128)S(1)}, f32[8,72]{1,0:T(8,128)}, u32[]{:S(2)}) %copy-start.6) | copy-done | bytes 2328
  7.2 0.0 copy-start.7
  7.2 0.7 %copy-done.7 = f32[8,72]{1,0:T(8,128)S(1)} copy-done((f32[8,72]{1,0:T(8,128)S(1)}, f32[8,72]{1,0:T(8,128)}, u32[]{:S(2)}) %copy-start.7) | copy-done | bytes 2328
  7.8 0.0 copy-start.8
  7.9 0.7 copy-done.8
  8.5 58.4 %step.1 = (f32[2,72,128]{2,1,0:T(8,128)S(1)}, f32[2,72,128]{2,1,0:T(8,128)S(1)}, bf16[1,2,2304,128]{3,2,1,0:T(8,128)(2,1)S(1)}, f32[2,32,128]{2,1,0:T(8,128)S(1)...) custom-call(s32[24]{0:T(128)S(1)} %copy-done.8, bf16[1,2,2304,128]{3,2,1,0:T(8,128)(2,1)S(1)} %copy-done, ...), custom_call_target="tpu_custom_call" | custom-call | tf_op jit(solution)/shard_map/step/pallas_call | solution.py:325
  66.9 1.1 %move.1 = (f32[2,72,128]{2,1,0:T(8,128)}, f32[2,72,128]{2,1,0:T(8,128)}, bf16[1,2,2304,128]{3,2,1,0:T(8,128)(2,1)}, f32[2,32,128]{2,1,0:T(8,128)}, f32[8,72]{1,0:T(8,128)}, /*index=5*/f32[8,72]{1,0:T(8,128)}) custom-call(f32[2,72,128]{2,1,0:T(8,128)S(1)} %get-tuple-element.18.refs_0_, f32[2,72,128]{2,1,0:T(8,128)S(1)} %get-tuple-element.19.refs_1_, ...), custom_call_target="tpu_custom_call" | custom-call | tf_op jit(solution)/shard_map/move/pallas_call | solution.py:346
Async XLA Ops:
  0.6 1.3 %copy-start = (bf16[1,2,2304,128]{3,2,1,0:T(8,128)(2,1)S(1)}, bf16[1,2,2304,128]{3,2,1,0:T(8,128)(2,1)}, u32[]{:S(2)}) copy-start(bf16[1,2,2304,128]{3,2,1,0:T(8,128)(2,1)} %grad_ref.1) | copy-start | bytes 3538948
  1.9 1.3 %copy-start.1 = (bf16[1,2,2304,128]{3,2,1,0:T(8,128)(2,1)S(1)}, bf16[1,2,2304,128]{3,2,1,0:T(8,128)(2,1)}, u32[]{:S(2)}) copy-start(bf16[1,2,2304,128]{3,2,1,0:T(8,128)(2,1)} %err_ref.1) | copy-start | bytes 3538948
  3.2 0.9 %copy-start.2 = (f32[2,72,128]{2,1,0:T(8,128)S(1)}, f32[2,72,128]{2,1,0:T(8,128)}, u32[]{:S(2)}) copy-start(f32[2,72,128]{2,1,0:T(8,128)} %w_ref.1) | copy-start | bytes 221188
  4.1 0.9 %copy-start.3 = (f32[2,72,128]{2,1,0:T(8,128)S(1)}, f32[2,72,128]{2,1,0:T(8,128)}, u32[]{:S(2)}) copy-start(f32[2,72,128]{2,1,0:T(8,128)} %m_ref.1) | copy-start | bytes 221188
  4.9 0.8 %copy-start.4 = (bf16[1,8,2304]{2,1,0:T(8,128)(2,1)S(1)}, bf16[1,8,2304]{2,1,0:T(8,128)(2,1)}, u32[]{:S(2)}) copy-start(bf16[1,8,2304]{2,1,0:T(8,128)(2,1)} %vec_ref.1) | copy-start | bytes 110596
  5.7 0.8 %copy-start.5 = (f32[2,128,32]{1,2,0:T(8,128)S(1)}, f32[2,128,32]{1,2,0:T(8,128)}, u32[]{:S(2)}) copy-start(f32[2,128,32]{1,2,0:T(8,128)} %param.12) | copy-start | bytes 98308
  6.5 0.7 %copy-start.6 = (f32[8,72]{1,0:T(8,128)S(1)}, f32[8,72]{1,0:T(8,128)}, u32[]{:S(2)}) copy-start(f32[8,72]{1,0:T(8,128)} %vw_ref.1) | copy-start | bytes 6916
  7.2 0.7 %copy-start.7 = (f32[8,72]{1,0:T(8,128)S(1)}, f32[8,72]{1,0:T(8,128)}, u32[]{:S(2)}) copy-start(f32[8,72]{1,0:T(8,128)} %vm_ref.1) | copy-start | bytes 6916
  7.8 0.7 copy-start.8

commit v4 on v3

--- a/solution.py
+++ b/solution.py
@@ -17,6 +17,7 @@
 HIGH = lax.Precision.HIGHEST
 XFAR = (2, 1, 3)
 YFAR = (4, 3, 5, 2, 6, 1, 7)
+YNEAR = (1, 7, 2, 6, 3, 5, 4)
 OFAR = (8, 7, 9, 6, 10, 5, 11, 4, 12, 3, 13, 2, 14, 1, 15)
 
 
@@ -32,8 +33,8 @@
 def step_kernel(
     own_ref, grad_ref, err_ref, q_ref, vec_ref, w_ref, m_ref, vw_ref, vm_ref,
     wn_ref, mn_ref, en_ref, qn_ref, vwn_ref, vmn_ref,
-    gv, ev, qv, vv, wv, mv, vwv, vmv, loc, pf, rx0, a0, ry0, ry1, c1, rx1, own1, gx1,
-    vpk, vrx, vc, vry, vqy, vqx, tt, try_, tx, tf, sc,
+    gv, ev, qv, vv, wv, mv, vwv, vmv, loc, pf, pc, rx0, a0, ry0,
+    vpk, vrx, vc, vry, vqy, vqx, tt, try_, tx, tf, sc, env,
     load_sem, send_sem, recv_sem,
     *, entries,
 ):
@@ -100,7 +101,9 @@
             part = slice(576 * j, 576 * j + 576)
             term = dot(jnp.concatenate([gv[s, part], ev[s, part]], axis=1), rhs)
             total = term if total is None else total + term
-        loc[576 * s:576 * s + 576] = total[:, :128] + total[:, 128:]
+        total = total[:, :128] + total[:, 128:]
+        for i in range(16):
+            loc[16 * s + i] = total[36 * i:36 * i + 36]
 
     loads[0].wait()
     loads[3].wait()
@@ -111,13 +114,10 @@
     left(0)
     pl.semaphore_wait(barrier, len(peers))
 
-    x0, y1 = [], []
-    for n in range(7):
-        to = lax.rem(y + YFAR[n], NY)
-        y1.append(send(loc.at[rows(768 + to * 48, 48)], ry1.at[YFAR[n] - 1], ypeer(YFAR[n])))
-        if n < 3:
-            to = lax.rem(x + XFAR[n], NX)
-            x0.append(send(loc.at[rows(to * 192, 192)], rx0.at[XFAR[n] - 1], xpeer(XFAR[n])))
+    x0 = []
+    for k, e in enumerate(YFAR + (0,)):
+        to_y = lax.rem(y + e, NY)
+        x0.append([send(loc.at[lax.rem(x + d, NX) * NY + to_y], rx0.at[d - 1, k], xpeer(d)) for d in XFAR])
 
     for load in loads[5:]:
         load.wait()
@@ -127,46 +127,30 @@
             at = 72 * (NX * yy + xx)
             vpk[xx * NY + yy] = jnp.concatenate([vall[:, at:at + 72], jnp.zeros((8, 56), f32)], axis=1)
 
-    arrive(x0)
-    a0[...] = loc[rows(x * 192, 192)] + rx0[0] + rx0[1] + rx0[2]
-    y0 = [send(a0.at[rows(lax.rem(y + d, NY) * 24, 24)], ry0.at[d - 1], ypeer(d)) for d in YFAR]
-
-    arrive(y1)
-    acc = loc[rows(768 + y * 48, 48)]
-    for d in range(7):
-        acc = acc + ry1[d]
-    pad4 = jnp.zeros((4, 128), f32)
-    for xx in range(NX):
-        c1[xx] = jnp.concatenate([acc[12 * xx:12 * xx + 12], pad4], axis=0)
-    x1 = [send(c1.at[lax.rem(x + d, NX)], rx1.at[d - 1], xpeer(d)) for d in XFAR]
+    y0 = []
+    for k, e in enumerate(YFAR + (0,)):
+        arrive(x0[k])
+        acc = (loc[x * NY + lax.rem(y + e, NY)] + rx0[0, k]) + (rx0[1, k] + rx0[2, k])
+        if e:
+            a0[k] = acc
+            y0.append(send(a0.at[k], ry0.at[e - 1], ypeer(e)))
     vx = [send(vpk.at[pl.ds(lax.rem(x + d, NX) * NY, NY)], vrx.at[d - 1], xpeer(d)) for d in XFAR]
 
-    arrive(x1)
-    acc = c1[x] + rx1[0] + rx1[1] + rx1[2]
-    own1[...] = acc
-    gx1[x] = acc
-    g1 = [send(own1, gx1.at[x], xpeer(d)) for d in XFAR]
-
     arrive(y0)
-    acc = a0[rows(y * 24, 24)]
     for d in range(7):
         acc = acc + ry0[d]
-    mine = rows(x * 192 + y * 24, 24)
+    mine = x * NY + y
     pf[mine] = acc
-    g0 = [send(pf.at[mine], pf.at[mine], ypeer(d)) for d in YFAR]
-
-    arrive(g1)
-    block1 = rows(768 + y * 48, 48)
-    pf[block1] = jnp.concatenate([gx1[xx, 0:12] for xx in range(NX)], axis=0)
-    h1 = [send(pf.at[block1], pf.at[block1], ypeer(d)) for d in YFAR]
+    g0 = {e: send(pf.at[mine], pf.at[mine], ypeer(e)) for e in YFAR}
+    h0 = [send(pf.at[mine], pf.at[mine], xpeer(d)) for d in XFAR]
+    for e in YNEAR:
+        arrive([g0[e]])
+        block = x * NY + lax.rem(y + NY - e, NY)
+        h0 += [send(pf.at[block], pf.at[block], xpeer(d)) for d in XFAR]
 
     arrive(vx)
     vc[...] = vpk[pl.ds(x * NY, NY)] + vrx[0] + vrx[1] + vrx[2]
     vy = [send(vc.at[lax.rem(y + d, NY)], vry.at[d - 1], ypeer(d)) for d in YFAR]
-
-    arrive(g0)
-    block0 = rows(x * 192, 192)
-    h0 = [send(pf.at[block0], pf.at[block0], xpeer(d)) for d in XFAR]
 
     arrive(vy)
     vsum = vc[y]
@@ -176,7 +160,9 @@
     vqy[y] = jnp.sum(vmean * vmean, axis=0, keepdims=True)
 
     def right(s):
-        hi, lo = split(pf[576 * s:576 * s + 576])
+        p = jnp.concatenate([pf[16 * s + i] for i in range(16)], axis=0)
+        pc[576 * s:576 * s + 576] = p
+        hi, lo = split(p)
         lhs = jnp.concatenate([hi, lo], axis=1)
         total = None
         for j in range(4):
@@ -190,7 +176,6 @@
 
     arrive(h0)
     right(0)
-    arrive(h1)
     right(1)
     ty = [send(tt.at[lax.rem(y + d, NY)], try_.at[d - 1], ypeer(d)) for d in YFAR]
     qy = [send(vqy.at[y], vqy.at[y], ypeer(d)) for d in YFAR]
@@ -200,7 +185,7 @@
 
     grams = []
     for s in range(2):
-        p = pf[576 * s:576 * s + 576]
+        p = pc[576 * s:576 * s + 576]
         wide = jnp.where(row_block == lane_block, dot(p, p, ((0,), (0,)), HIGH), 0.0)
         g = (wide[0:32] + wide[32:64]) + (wide[64:96] + wide[96:128])
         g = g + pltpu.roll(g, 64, 1)
@@ -260,7 +245,7 @@
     sc[o] = jnp.sum(qt * pq * live_row, axis=0, keepdims=True) + vtot
     s1 = [send(sc.at[o], sc.at[o], opeer(d)) for d in OFAR]
 
-    approx_rows = []
+    approx_rows, puts = [], []
     for s in range(2):
         live = s < count
         hi, lo = split(jnp.concatenate([b[32 * s:32 * s + 32]] * 4, axis=0))
@@ -273,11 +258,14 @@
 
         for j in range(4):
             part = slice(576 * j, 576 * j + 576)
-            approx = product(pf[576 * s:576 * s + 576], row_block == j)
+            approx = product(pc[576 * s:576 * s + 576], row_block == j)
             e = ev[s, part]
             merged = gv[s, part].astype(f32) + e.astype(f32)
-            en_ref[0, s, part] = jnp.where(live, (merged - approx).astype(bf16), e)
-        approx_rows.append(product(pf[rows(576 * s + lax.rem(r, 8) * 72, 72)], row_block == r // 8))
+            env[s, part] = jnp.where(live, (merged - approx).astype(bf16), e)
+        approx_rows.append(product(pc[rows(576 * s + lax.rem(r, 8) * 72, 72)], row_block == r // 8))
+        put = pltpu.make_async_copy(env.at[s], en_ref.at[0, s], load_sem.at[10 + s])
+        put.start()
+        puts.append(put)
         qn_ref[s] = jnp.where(live, qt[32 * s:32 * s + 32], qv[s])
 
     arrive(s1)
@@ -295,17 +283,27 @@
     vmn = momentum_decay * vmv[...] + fac * vmean[:, :72]
     vmn_ref[...] = vmn
     vwn_ref[...] = vwv[...] - learn_rate * vmn
+    for put in puts:
+        put.wait()
     for copy in started:
         copy.wait_send()
 
 
 def move_kernel(*refs):
-    n = len(refs) // 2
-    copies = [pltpu.make_async_copy(refs[i], refs[n + i], refs[2 * n].at[i]) for i in (2, 0, 1, 3, 4, 5)]
-    for copy in copies:
-        copy.start()
-    for copy in copies:
-        copy.wait()
+    src, dst, held = refs[0:6], refs[6:12], refs[12:18]
+    in_sem, out_sem = refs[18:]
+    parts = [(2, (0, i, pl.ds(1152 * h, 1152))) for i in range(2) for h in range(2)]
+    parts += [(i, (Ellipsis,)) for i in (0, 1, 3, 4, 5)]
+    loads, puts = [], []
+    for n, (i, at) in enumerate(parts):
+        loads.append(pltpu.make_async_copy(src[i].at[at], held[i].at[at], in_sem.at[n]))
+        puts.append(pltpu.make_async_copy(held[i].at[at], dst[i].at[at], out_sem.at[n]))
+        loads[-1].start()
+    for load, put in zip(loads, puts):
+        load.wait()
+        put.start()
+    for put in puts:
+        put.wait()
 
 
 def on_device(owner_of, grad, error, q_prev, weight, momentum, vec_grad, vec_weight, vec_mom):
@@ -315,7 +313,7 @@
     smem = pl.BlockSpec(memory_space=pltpu.SMEM)
     width = grad.shape[2]
     entries = float(owner_of.shape[0] * width * grad.shape[3] + NO * vec_grad.shape[1] * width)
-    n_sends = 3 + 7 + 7 + 3 + 3 + 3 + 7 + 7 + 7 + 3 + 7 + 7 + 3 + 3 + 7 + 15
+    n_sends = 24 + 7 + 3 + 7 + 24 + 7 + 7 + 7 + 3 + 3 + 7 + 15
     V = pltpu.VMEM
     q_rows = jnp.swapaxes(q_prev, 1, 2)
     shapes = (
@@ -326,30 +324,29 @@
         functools.partial(step_kernel, entries=entries),
         out_shape=shapes,
         in_specs=[smem] + [hbm] * 8,
-        out_specs=(vm,) * 6,
+        out_specs=(vm, vm, hbm, vm, vm, vm),
         scratch_shapes=[
             V((2, 2304, 128), bf16), V((2, 2304, 128), bf16), V((2, 32, 128), f32), V((8, 2304), bf16),
             V((2, 72, 128), f32), V((2, 72, 128), f32), V((8, 72), f32), V((8, 72), f32),
-            V((1152, 128), f32), V((1152, 128), f32),
-            V((3, 192, 128), f32), V((192, 128), f32), V((7, 24, 128), f32),
-            V((7, 48, 128), f32), V((4, 16, 128), f32), V((3, 16, 128), f32), V((16, 128), f32), V((4, 16, 128), f32),
+            V((32, 36, 128), f32), V((32, 36, 128), f32), V((1152, 128), f32),
+            V((3, 8, 36, 128), f32), V((7, 36, 128), f32), V((7, 36, 128), f32),
             V((32, 8, 128), f32), V((3, 8, 8, 128), f32), V((8, 8, 128), f32), V((7, 8, 128), f32),
             V((8, 1, 128), f32), V((4, 1, 128), f32),
             V((8, 8, 128), f32), V((7, 8, 128), f32), V((4, 8, 128), f32), V((8, 8, 128), f32), V((16, 1, 128), f32),
-            pltpu.SemaphoreType.DMA((10,)),
+            V((2, 2304, 128), bf16),
+            pltpu.SemaphoreType.DMA((12,)),
             pltpu.SemaphoreType.DMA((n_sends,)),
             pltpu.SemaphoreType.DMA((n_sends,)),
         ],
-        compiler_params=pltpu.CompilerParams(collective_id=0, has_side_effects=True, vmem_limit_bytes=24 << 20),
+        compiler_params=pltpu.CompilerParams(collective_id=0, has_side_effects=True),
         name="step",
     )(owner_of, grad, error, q_rows, vec_grad, weight, momentum, vec_weight, vec_mom)
     wn, mn, en, qn, vwn, vmn = pl.pallas_call(
         move_kernel,
         out_shape=shapes,
-        in_specs=[vm] * 6,
+        in_specs=[hbm] * 6,
         out_specs=(hbm,) * 6,
-        scratch_shapes=[pltpu.SemaphoreType.DMA((6,))],
-        compiler_params=pltpu.CompilerParams(vmem_limit_bytes=8 << 20),
+        scratch_shapes=[V(t.shape, t.dtype) for t in shapes] + [pltpu.SemaphoreType.DMA((9,))] * 2,
         name="move",
     )(*results)
     return wn, mn, en, jnp.swapaxes(qn, 1, 2), vwn, vmn

time: 68.5 us -> 62.2 us (0.908)
  local copies, waits for them, and re-layouts: 7.85 us -> 0 us
  Pallas kernels: 59.5 us -> 61.4 us
    unnamed x18 -> x0, local copies, waits for them, and re-layouts: 7.85 us -> none
    pallas_call x1, Pallas kernels: 1.11 us -> 2.18 us  [on_device(): pl.pallas_call(move_kernel, out_shape=shapes, in_specs=[hbm] * 6, out_spe...]
    pallas_call x1, Pallas kernels: 58.4 us -> 59.2 us  [on_device(): pl.pallas_call(functools.partial(step_kernel, entries=entries), out_shape...]
where the time goes in v4:
time: 62.2 us; the launch traced here: 62 us
  Pallas kernels  61.4 us (99%)
  between operations  0.64 us (1%)
    pallas_call x1, Pallas kernels, on_device(): pl.pallas_call(functools.partial(step_kernel, entries=entries), out_shape...  59.2 us
    pallas_call x1, Pallas kernels, on_device(): pl.pallas_call(move_kernel, out_shape=shapes, in_specs=[hbm] * 6, out_spe...  2.18 us

profile of v4, /device:TPU:1, one launch (start us, length us, event | category | flops | bytes accessed | tf_op | source)
XLA Modules:
  0.0 62.0 jit_solution(3089054040713201687)
XLA Ops:
  0.6 59.2 %step.1 = (f32[2,72,128]{2,1,0:T(8,128)}, f32[2,72,128]{2,1,0:T(8,128)}, bf16[1,2,2304,128]{3,2,1,0:T(8,128)(2,1)}, f32[2,32,128]{2,1,0:T(8,128)}, f32[8,72]{1,0:T(8,128)}, /*index=5*/f32[8,72]{1,0:T(8,128)}) custom-call(s32[24]{0:T(128)} %own_ref.1, bf16[1,2,2304,128]{3,2,1,0:T(8,128)(2,1)} %grad_ref.1, bf16[1,2,2304,128]{3,2,1,0:T(8,128)(2,1)} %err_ref.1, ...), custom_call_target="tpu_custom_call" | custom-call | tf_op jit(solution)/shard_map/step/pallas_call | solution.py:323
  59.9 2.2 %move.1 = (f32[2,72,128]{2,1,0:T(8,128)}, f32[2,72,128]{2,1,0:T(8,128)}, bf16[1,2,2304,128]{3,2,1,0:T(8,128)(2,1)}, f32[2,32,128]{2,1,0:T(8,128)}, f32[8,72]{1,0:T(8,128)}, /*index=5*/f32[8,72]{1,0:T(8,128)}) custom-call(f32[2,72,128]{2,1,0:T(8,128)} %get-tuple-element.18.refs_0_, f32[2,72,128]{2,1,0:T(8,128)} %get-tuple-element.19.refs_1_, ...), custom_call_target="tpu_custom_call" | custom-call | tf_op jit(solution)/shard_map/move/pallas_call | solution.py:344
